TPU v7x, 32 devices: a whole 2x2x4 slice. The times are simulated.
32 devices in a mesh: seq: 8 (over z, x), vocab: 4 (over y, core).
Axes of the slice: x: 2, y: 2, z: 4, core: 2. Of those that a mesh axis runs over, the one named last changes fastest.
Arguments:
- rollout: bfloat16 [288, 4096], P('seq')
- group_count: int32 [8], replicated, may hold values from 12 to 36, as said below
- final_gain: float32 [4096], replicated, may hold values from 0.5 to 1.5
- head_weight: bfloat16 [4096, 152064], P(None, ('seq', 'vocab'))
- teacher_index: int32 [192, 64], replicated, may hold values from 0 to 152063, as said below
- teacher_logprob: float32 [192, 64], replicated, as said below
Outputs:
- kl: float32 [192], P('seq')
- grad_weight: bfloat16 [4096, 152064], P(None, ('seq', 'vocab'))
- grad_rollout: bfloat16 [288, 4096], P('seq', 'vocab')
Inputs may be any that keep to these rules, and one draw needn't show every extreme that they name: The first group_count[g] of the 36 slots of group g are live, the rest padding; the counts sum to 192. `teacher_index`: the 64 ids of one token are distinct. `teacher_logprob`: the exponentials of one token's entries sum to less than 1.
All inputs are finite; a program needn't handle non-finite values.
Results may differ from a plain program's by a relative error of at most 0.0075.
Values may be sent and summed in bfloat16 or wider, within the bound.
A program may use at most 128 MiB of HBM per device.

v0:
```python
import jax
import jax.numpy as jnp
from jax import lax
from jax.sharding import PartitionSpec as P

norm_eps = 1e-06
loss_scale = 16.0


def per_device(rollout, group_count, final_gain, head_weight, teacher_index, teacher_logprob):
    groups = lax.axis_size("seq")
    gen_slots, feature_width = rollout.shape
    tokens = teacher_index.shape[0]
    pack_rows = tokens // groups
    capacity = -(-gen_slots // groups)
    own_index = lax.axis_index("seq")
    offsets = jnp.cumsum(group_count) - group_count
    own_offset = offsets[own_index]
    own_count = group_count[own_index]
    row_ids = jnp.arange(capacity * groups, dtype=jnp.int32)
    padded = jnp.pad(rollout, ((0, capacity * groups - gen_slots), (0, 0)))
    padded = jnp.where((row_ids < own_count)[:, None], padded, jnp.zeros_like(padded))
    outgoing = jnp.roll(padded.reshape(capacity, groups, feature_width), own_offset, axis=1)
    arriving = lax.all_to_all(outgoing, "seq", split_axis=1, concat_axis=1, tiled=True)
    slot_ids = jnp.arange(capacity, dtype=jnp.int32)[:, None]
    row_in_group = slot_ids * groups + (own_index - offsets[None, :]) % groups
    is_live = row_in_group < group_count[None, :]
    position = jnp.where(is_live, (offsets[None, :] + row_in_group) // groups, pack_rows)
    packed = jnp.zeros((pack_rows, feature_width), rollout.dtype)
    packed = packed.at[position.reshape(-1)].set(arriving.reshape(-1, feature_width), mode="drop")
    values = packed.astype(jnp.float32)
    inv_rms = lax.rsqrt(jnp.mean(values * values, axis=1, keepdims=True) + norm_eps)
    normed = (values * inv_rms * final_gain).astype(jnp.bfloat16)
    all_rows = lax.all_gather(normed, "seq", axis=0, tiled=True)
    logits = jnp.dot(all_rows, head_weight, preferred_element_type=jnp.float32)
    vocab_dev = head_weight.shape[1]
    first_column = lax.axis_index(("seq", "vocab")) * vocab_dev
    local_index = teacher_index - first_column
    owned = (local_index >= 0) & (local_index < vocab_dev)
    teacher_prob = jnp.exp(teacher_logprob)
    teacher_mass = jnp.sum(teacher_prob, axis=1)
    token_ids = jnp.arange(tokens, dtype=jnp.int32)[:, None]
    column = jnp.where(owned, local_index, vocab_dev)
    teacher_dense = (
        jnp.zeros((tokens, vocab_dev), jnp.float32)
        .at[token_ids, column]
        .add(teacher_prob, mode="drop")
    )
    target_part = jnp.sum(teacher_dense * logits, axis=1)
    local_peak = jnp.max(logits, axis=1)
    row_peak = lax.pmax(local_peak, ("seq", "vocab"))
    local_total = jnp.sum(jnp.exp(logits - row_peak[:, None]), axis=1)
    row_total, target_sum = lax.psum((local_total, target_part), ("seq", "vocab"))
    log_total = row_peak + jnp.log(row_total)
    kl_all = jnp.sum(teacher_prob * teacher_logprob, axis=1) - target_sum + teacher_mass * log_total
    kl = lax.dynamic_slice_in_dim(kl_all, own_index * pack_rows, pack_rows)
    student_part = teacher_mass[:, None] * jnp.exp(logits - log_total[:, None]) - teacher_dense
    grad_logits = (loss_scale * student_part).astype(jnp.bfloat16)
    grad_weight = lax.dot_general(
        all_rows, grad_logits, (((0,), (0,)), ((), ())), preferred_element_type=jnp.float32
    ).astype(jnp.bfloat16)
    share = feature_width // lax.axis_size("vocab")
    feature_start = lax.axis_index("vocab") * share
    x_share = lax.dynamic_slice_in_dim(values, feature_start, share, 1)
    partial_rows = lax.psum_scatter(
        lax.dot_general(
            grad_logits, head_weight, (((1,), (1,)), ((), ())), preferred_element_type=jnp.float32
        ),
        "seq",
        scatter_dimension=0,
        tiled=True,
    )
    whole_rows = lax.psum(partial_rows, "vocab")
    full_grad = whole_rows * final_gain
    row_dots = jnp.sum(full_grad * values, axis=1, keepdims=True)
    scaled_grad = lax.dynamic_slice_in_dim(full_grad, feature_start, share, 1)
    grad_packed = (
        (scaled_grad - x_share * inv_rms * inv_rms * row_dots / feature_width) * inv_rms
    ).astype(jnp.bfloat16)
    taken = jnp.take(grad_packed, jnp.minimum(position, pack_rows - 1), axis=0)
    outgoing_back = jnp.where(is_live[:, :, None], taken, jnp.zeros_like(taken))
    coming_back = lax.all_to_all(outgoing_back, "seq", split_axis=1, concat_axis=1, tiled=True)
    restored = jnp.roll(coming_back, -own_offset, axis=1).reshape(capacity * groups, share)
    grad_rollout = restored[:gen_slots]
    return (kl, grad_weight, grad_rollout)


def solution(mesh):
    placed = (P("seq", None), P(), P(), P(None, ("seq", "vocab")), P(), P())
    return jax.shard_map(
        per_device,
        mesh=mesh,
        in_specs=placed,
        out_specs=(P("seq"), P(None, ("seq", "vocab")), P("seq", "vocab")),
        check_vma=False,
    )
```

profile of v0, /device:TPU:0, one launch (start us, length us, event | category | flops | bytes accessed | tf_op | source)
XLA Modules:
  0.0 382.8 jit_solution(6932193462676987082)
XLA Ops:
  7.2 1.3 dynamic_slice.23
  8.5 0.8 reduce-window.9
  9.3 0.7 and_select_fusion.1
  10.0 0.6 dynamic_slice.24
  12.5 0.7 iota_compare_fusion
  13.2 1.1 select_bitcast_fusion
  14.3 0.2 fusion.2
  14.6 1.0 copy.18
  15.5 7.3 %all-to-all-start = ((bf16[5,8,4096]{2,0,1:T(8,128)(2,1)}), bf16[5,8,4096]{2,0,1:T(8,128)(2,1)S(1)}, u32[]{:S(2)}, u32[]{:S(2)}) async-start(bf16[5,8,4096]{2,0,1:T(8,128)(2,1)} %copy.18), calls=%async_computation | async-start | bytes 1048576 | tf_op jit(solution)/shard_map/all_to_all | solution.py:24
  22.9 0.7 compare_and_fusion
  23.9 13.4 %all-to-all-done = bf16[5,8,4096]{2,0,1:T(8,128)(2,1)S(1)} async-done(((bf16[5,8,4096]{2,0,1:T(8,128)(2,1)}), bf16[5,8,4096]{2,0,1:T(8,128)(2,1)S(1)}, u32[]{:S(2)}, u32[]{:S(2)}) %all-to-all-start) | async-done | bytes 327712 | tf_op jit(solution)/shard_map/all_to_all | solution.py:24
  37.3 1.4 scatter_custom_fusion
  38.7 0.2 multiply_reduce_fusion.2
  38.9 0.8 multiply_convert_fusion.1
  39.9 0.1 and_reduce_fusion
  40.5 66.5 %scatter_custom_fusion.1 = f32[912384]{0:T(1024)} fusion(s32[12288]{0:T(1024)S(1)} %reshape.401, f32[12288]{0:T(1024)S(1)} %reshape.403, f32[]{:T(128)} %constant.100.clone.1), kind=kCustom, calls=%fused_computation.7 | custom fusion | flops 12288 | bytes 3649540
  107.0 5.8 %reshape.384 = f32[192,4752]{1,0:T(8,128)} reshape(f32[912384]{0:T(1024)} %scatter_custom_fusion.1) | data formatting | bytes 7299072 | tf_op jit(solution)/shard_map/scatter-add | solution.py:47
  112.7 20.6 %fusion.31 = (f32[192]{0:T(256)S(1)}, f32[192,4752]{1,0:T(8,128)}) fusion(bf16[192,4096]{1,0:T(8,128)(2,1)} %all-gather.2.cloned.1.call-done, bf16[4096,4752]{0,1:T(8,128)(2,1)} %param.9), kind=kOutput, calls=%fused_computation.86 | convolution fusion | flops 7475162112 | bytes 44151552 | tf_op jit(solution)/shard_map/dot_general | solution.py:35
  133.3 38.4 %pmax.7 = f32[192]{0:T(256)S(1)} all-reduce(f32[192]{0:T(256)S(1)} %get-tuple-element.18), channel_id=1, replica_groups=mesh['seq'=8,'vocab'=4] {'seq','vocab'}, use_global_device_ids=true, to_apply=%region_9.10 | all-reduce | flops 192 | bytes 1536 | tf_op jit(solution)/shard_map/pmax | solution.py:51
  171.7 4.2 %multiply_reduce_fusion = (f32[192]{0:T(256)S(1)}, f32[192]{0:T(256)S(1)}) fusion(f32[192,4752]{1,0:T(8,128)} %reshape.384, f32[192,4752]{1,0:T(8,128)} %get-tuple-element.19, f32[192]{0:T(256)S(1)} %pmax.7), kind=kLoop, calls=%fused_computation.6 | loop fusion | flops 3649152 | bytes 7301376 | tf_op jit(solution)/shard_map/reduce_sum | solution.py:49
  175.9 40.9 %all-reduce.1 = (f32[192]{0:T(256)S(1)}, f32[192]{0:T(256)S(1)}) all-reduce(f32[192]{0:T(256)S(1)} %get-tuple-element.4, f32[192]{0:T(256)S(1)} %get-tuple-element.3), channel_id=1, replica_groups=mesh['seq'=8,'vocab'=4] {'seq','vocab'}, use_global_device_ids=true, to_apply=%region_11.12 | all-reduce | flops 384 | bytes 3072 | tf_op jit(solution)/shard_map/psum | solution.py:53
  216.8 4.1 %multiply_convert_fusion = bf16[192,4752]{1,0:T(8,128)(2,1)S(1)} fusion(f32[192,4752]{1,0:T(8,128)} %reshape.384, f32[192,4752]{1,0:T(8,128)} %get-tuple-element.19, f32[192]{0:T(256)S(1)} %get-tuple-element.12, f32[192]{0:T(256)S(1)} %get-tuple-element.6), kind=kLoop, calls=%fused_computation.4 | loop fusion | flops 4561920 | bytes 9125376 | tf_op jit(solution)/shard_map/convert_element_type | solution.py:58
  220.9 18.2 %fusion.32 = f32[192,4096]{1,0:T(8,128)} fusion(bf16[192,4752]{1,0:T(8,128)(2,1)S(1)} %multiply_convert_fusion, bf16[4096,4752]{0,1:T(8,128)(2,1)} %param.9), kind=kOutput, calls=%fused_computation.87 | convolution fusion | flops 7474249728 | bytes 43898880 | tf_op jit(solution)/shard_map/dot_general | solution.py:66
  239.3 74.6 %reduce-scatter.2.cloned.1.call-done = f32[24,4096]{1,0:T(8,128)} async-done(((f32[192,4096]{1,0:T(8,128)}), f32[24,4096]{1,0:T(8,128)}) %reduce-scatter.2.cloned.1.call-update) | async-done | bytes 393232 | tf_op jit(solution)/shard_map/reduce_scatter | solution.py:65
  315.0 33.2 %all-reduce.4.cloned.1.call-done = f32[24,4096]{1,0:T(8,128)} async-done(((f32[24,4096]{1,0:T(8,128)}), f32[24,4096]{1,0:T(8,128)}) %all-reduce.4.cloned.1.call-update) | async-done | bytes 393232 | tf_op jit(solution)/shard_map/psum | solution.py:73
  348.2 1.2 multiply_reduce_fusion.1
  349.4 0.7 gather_fusion
  350.1 0.7 fusion.6
  350.8 5.5 %all-to-all-start.1 = ((bf16[5,8,1024]{2,0,1:T(8,128)(2,1)}), bf16[5,8,1024]{2,0,1:T(8,128)(2,1)S(1)}, u32[]{:S(2)}, u32[]{:S(2)}) async-start(bf16[5,8,1024]{2,0,1:T(8,128)(2,1)} %fusion.6), calls=%async_computation.2 | async-start | bytes 262144 | tf_op jit(solution)/shard_map/all_to_all | solution.py:82
  356.3 18.6 %convolution_convert_fusion = bf16[4096,4752]{0,1:T(8,128)(2,1)} fusion(bf16[192,4096]{1,0:T(8,128)(2,1)} %all-gather.2.cloned.1.call-done, bf16[192,4752]{1,0:T(8,128)(2,1)S(1)} %multiply_convert_fusion), kind=kOutput, calls=%fused_computation.3 | convolution fusion | flops 7493713920 | bytes 42326016 | tf_op jit(solution)/shard_map/dot_general | solution.py:59
  374.9 0.6 dynamic_slice.26
  375.6 0.7 fusion.9
  (44 shorter events, 1.5 us)
Async XLA Ops:
  7.2 32.7 %copy-start.5 = (s32[2]{0:T(128)S(1)}, s32[2]{0:T(128)}, u32[]{:S(2)}) copy-start(s32[2]{0:T(128)} %constant.127) | copy-start | bytes 28
  7.2 32.8 %copy-start.4 = (s32[2]{0:T(128)S(1)}, s32[2]{0:T(128)}, u32[]{:S(2)}) copy-start(s32[2]{0:T(128)} %constant.130) | copy-start | bytes 28
  7.2 31.7 %copy-start = (f32[4096]{0:T(1024)S(1)}, f32[4096]{0:T(1024)}, u32[]{:S(2)}) copy-start(f32[4096]{0:T(1024)} %param.8) | copy-start | bytes 49156
  7.2 32.6 %copy-start.1 = (s32[192,64]{0,1:T(8,128)S(1)}, s32[192,64]{0,1:T(8,128)}, u32[]{:S(2)}) copy-start(s32[192,64]{0,1:T(8,128)} %param.10) | copy-start | bytes 147460
  7.2 33.0 %copy-start.2 = (f32[192,64]{0,1:T(8,128)S(1)}, f32[192,64]{0,1:T(8,128)}, u32[]{:S(2)}) copy-start(f32[192,64]{0,1:T(8,128)} %param.11) | copy-start | bytes 147460
  15.5 21.8 %all-to-all-start = ((bf16[5,8,4096]{2,0,1:T(8,128)(2,1)}), bf16[5,8,4096]{2,0,1:T(8,128)(2,1)S(1)}, u32[]{:S(2)}, u32[]{:S(2)}) async-start(bf16[5,8,4096]{2,0,1:T(8,128)(2,1)} %copy.18), calls=%async_computation | async-start | bytes 1048576 | tf_op jit(solution)/shard_map/all_to_all | solution.py:24
  22.8 89.9 %all-gather.2.cloned.1.call-start = ((), (), s32[]{:S(2)}) async-start(), calls=%async_computation.3 | async-start | bytes 1769472 | tf_op jit(solution)/shard_map/all_gather | solution.py:34
  39.7 274.2 %reduce-scatter.2.cloned.1.call-start = ((), (), s32[]{:S(2)}) async-start(), calls=%async_computation.4 | async-start | bytes 3538944 | tf_op jit(solution)/shard_map/reduce_scatter | solution.py:65
  220.9 93.0 %copy-start.3 = (s32[8]{0:T(128)S(1)}, s32[8]{0:T(128)}, u32[]{:S(2)}) copy-start(s32[8]{0:T(128)} %param.7) | copy-start | bytes 100
  239.2 109.0 %all-reduce.4.cloned.1.call-start = ((), (), s32[]{:S(2)}) async-start(), calls=%async_computation.5 | async-start | bytes 786432 | tf_op jit(solution)/shard_map/psum | solution.py:73
  350.8 24.7 %all-to-all-start.1 = ((bf16[5,8,1024]{2,0,1:T(8,128)(2,1)}), bf16[5,8,1024]{2,0,1:T(8,128)(2,1)S(1)}, u32[]{:S(2)}, u32[]{:S(2)}) async-start(bf16[5,8,1024]{2,0,1:T(8,128)(2,1)} %fusion.6), calls=%async_computation.2 | async-start | bytes 262144 | tf_op jit(solution)/shard_map/all_to_all | solution.py:82
Sparse Core Ops, SparseCore 0:
  39.8 43.2 all-gather.1
  239.3 74.4 reduce-scatter.1
  316.2 31.8 all-reduce.3
where the time goes:
time: 384 us; the launch traced here: 383 us
  waiting for transfers between devices  121 us (32%)
  other arithmetic  83.2 us (22%)
  blocking collectives  79.3 us (21%)
  matrix products  57.5 us (15%)
  between operations  16.6 us (4%)
  starting transfers between devices  12.9 us (3%)
  local copies, waits for them, and re-layouts  12.1 us (3%)
    reduce_scatter x1, waiting for transfers between devices, per_device(): lax.psum_scatter(lax.dot_general(grad_logits, head_weight, (((1,), (1,)),...  74.6 us
    unnamed x4, other arithmetic  66.7 us
    psum x1, blocking collectives, per_device(): lax.psum((local_total, target_part), ('seq', 'vocab'))  40.9 us
    pmax x1, blocking collectives, per_device(): row_peak = lax.pmax(local_peak, ('seq', 'vocab'))  38.4 us
    psum x1, waiting for transfers between devices, per_device(): whole_rows = lax.psum(partial_rows, 'vocab')  33.2 us
    dot_general x1, matrix products, per_device(): logits = jnp.dot(all_rows, head_weight, preferred_element_type=jnp.float32)  20.6 us
    dot_general x1, matrix products, per_device(): lax.dot_general(all_rows, grad_logits, (((0,), (0,)), ((), ())), preferre...  18.6 us
    dot_general x1, matrix products, per_device(): lax.dot_general(grad_logits, head_weight, (((1,), (1,)), ((), ())), prefe...  18.2 us
  transfers between devices with their start and end apart: 5, of which 3 were waited for; matrix products, arithmetic and copies ran while one was open for 24% of the time, Pallas kernels for 0%

commit v1 on v0

v1 whole, which is shorter than its diff:
```python
import functools

import jax
import jax.numpy as jnp
from jax import lax
from jax.experimental import pallas as pl
from jax.experimental.pallas import tpu as pltpu
from jax.sharding import PartitionSpec as P

norm_eps = 1e-06
loss_scale = 16.0
VMEM = pltpu.VMEM
DMA = pltpu.SemaphoreType.DMA


def remote(src, dst, send, recv, where):
    return pltpu.make_async_remote_copy(
        src_ref=src,
        dst_ref=dst,
        send_sem=send,
        recv_sem=recv,
        device_id=where,
        device_id_type=pl.DeviceIdType.MESH,
    )


def greet_all(groups, shares):
    s, v = lax.axis_index("seq"), lax.axis_index("vocab")
    barrier = pltpu.get_barrier_semaphore()
    for k in range(1, shares):
        pl.semaphore_signal(
            barrier, inc=1, device_id=(s, lax.rem(v + k, shares)), device_id_type=pl.DeviceIdType.MESH
        )
    for k in range(1, groups):
        pl.semaphore_signal(
            barrier, inc=1, device_id=(lax.rem(s + k, groups), v), device_id_type=pl.DeviceIdType.MESH
        )
    pl.semaphore_wait(barrier, groups + shares - 2)
    return s, v


def dense_kernel(width, col_ref, prob_ref, out_ref):
    rows, entries = col_ref.shape
    step = 1280
    for start in range(0, width, step):
        size = min(step, width - start)
        ids = lax.broadcasted_iota(jnp.int32, (rows, size), 1) + start
        acc = jnp.zeros((rows, size), jnp.float32)
        for j in range(entries):
            acc = jnp.where(ids == col_ref[:, j : j + 1], prob_ref[:, j : j + 1], acc)
        out_ref[:, start : start + size] = acc


def teacher_table(column, prob, width):
    tokens, entries = column.shape
    return pl.pallas_call(
        functools.partial(dense_kernel, width),
        grid=(tokens // 8,),
        out_shape=jax.ShapeDtypeStruct((tokens, width), jnp.float32),
        in_specs=[pl.BlockSpec((8, entries), lambda i: (i, 0))] * 2,
        out_specs=pl.BlockSpec((8, width), lambda i: (i, 0)),
        cost_estimate=pl.CostEstimate(
            flops=tokens * entries * width, bytes_accessed=tokens * width * 40, transcendentals=0
        ),
    )(column, prob)


def merge_stats(ref, count):
    peak = ref[0, 0:1, :]
    for i in range(1, count):
        peak = jnp.maximum(peak, ref[i, 0:1, :])
    total = jnp.zeros_like(peak)
    target = jnp.zeros_like(peak)
    for i in range(count):
        total = total + ref[i, 1:2, :] * jnp.exp(ref[i, 0:1, :] - peak)
        target = target + ref[i, 2:3, :]
    return peak, total, target


def put_stats(ref, stats):
    for i in range(3):
        ref[i : i + 1, :] = stats[i]


def stats_kernel(groups, shares, in_ref, out_ref, near, far, send_a, recv_a, send_b, recv_b):
    s, v = greet_all(groups, shares)
    first = []
    for k in range(1, shares):
        first.append(
            remote(in_ref, near.at[v], send_a.at[k], recv_a.at[k], (s, lax.rem(v + k, shares)))
        )
        first[-1].start()
    near[v] = in_ref[...]
    for copy in first:
        copy.wait()
    put_stats(out_ref, merge_stats(near, shares))
    far[s] = out_ref[...]
    second = []
    for k in range(1, groups):
        second.append(
            remote(far.at[s], far.at[s], send_b.at[k], recv_b.at[k], (lax.rem(s + k, groups), v))
        )
        second[-1].start()
    for copy in second:
        copy.wait()
    put_stats(out_ref, merge_stats(far, groups))


def exchange_stats(stats, groups, shares):
    return pl.pallas_call(
        functools.partial(stats_kernel, groups, shares),
        out_shape=jax.ShapeDtypeStruct(stats.shape, stats.dtype),
        in_specs=[pl.BlockSpec(memory_space=VMEM)],
        out_specs=pl.BlockSpec(memory_space=VMEM),
        scratch_shapes=[
            VMEM((shares,) + stats.shape, jnp.float32),
            VMEM((groups,) + stats.shape, jnp.float32),
            DMA((shares,)),
            DMA((shares,)),
            DMA((groups,)),
            DMA((groups,)),
        ],
        compiler_params=pltpu.CompilerParams(collective_id=0, has_side_effects=True),
    )(stats)


def hidden_kernel(
    groups, shares, part_ref, place_ref, x_ref, inv_ref, gain_ref, out_ref,
    pair_in, held, cross_in, spread, rows_in, dots, dots_in,
    send_a, recv_a, send_b, recv_b, send_c, recv_c, send_d, recv_d,
):
    s, v = greet_all(groups, shares)
    width = part_ref.shape[1] // shares
    chips = shares // 2
    y, core = v // 2, lax.rem(v, 2)
    partner = (s, v + 1 - 2 * core)

    def columns(chip, side):
        return pl.ds(pl.multiple_of((2 * chip + side) * width, 128), width)

    order = list(range(1, chips)) + [0]
    pair = {}
    for k in order:
        chip = lax.rem(y + k, chips)
        pair[k] = remote(
            part_ref.at[:, columns(chip, 1 - core)], pair_in.at[k], send_a.at[k], recv_a.at[k], partner
        )
        pair[k].start()
    cross = []
    for k in range(1, chips):
        chip = lax.rem(y + k, chips)
        pair[k].wait()
        mine = part_ref[:, columns(chip, core)].astype(jnp.float32)
        held[k] = (mine + pair_in[k].astype(jnp.float32)).astype(jnp.bfloat16)
        copy = remote(
            held.at[k], cross_in.at[k], send_b.at[k], recv_b.at[k], (s, 2 * chip + core)
        )
        copy.start()
        cross.append(copy)
    pair[0].wait()
    total = part_ref[:, columns(y, core)].astype(jnp.float32) + pair_in[0].astype(jnp.float32)
    for k in range(1, chips):
        cross[k - 1].wait()
        total = total + cross_in[k].astype(jnp.float32)
    total = total.astype(jnp.bfloat16)
    back = []
    for k in range(1, groups):
        group = lax.rem(s + k, groups)
        spread[k] = jnp.dot(
            place_ref[group], total, preferred_element_type=jnp.float32
        ).astype(jnp.bfloat16)
        copy = remote(spread.at[k], rows_in.at[k], send_c.at[k], recv_c.at[k], (group, v))
        copy.start()
        back.append(copy)
    grad = jnp.dot(place_ref[s], total, preferred_element_type=jnp.float32)
    for k in range(1, groups):
        back[k - 1].wait()
        grad = grad + rows_in[k].astype(jnp.float32)
    x = x_ref[...].astype(jnp.float32)
    inv = inv_ref[...]
    u = grad * gain_ref[...]
    own_dots = jnp.sum(u * x, axis=1, keepdims=True)
    dots[...] = jnp.broadcast_to(own_dots, dots.shape)
    last = []
    for k in range(1, shares):
        copy = remote(dots, dots_in.at[k], send_d.at[k], recv_d.at[k], (s, lax.rem(v + k, shares)))
        copy.start()
        last.append(copy)
    row_dots = own_dots
    for k in range(1, shares):
        last[k - 1].wait()
        row_dots = row_dots + dots_in[k][:, 0:1]
    features = width * shares
    out_ref[...] = ((u - x * inv * inv * row_dots / features) * inv).astype(jnp.bfloat16)


def reduce_hidden(part, place, x, inv, gain, groups, shares):
    tokens, features = part.shape
    slots, width = x.shape
    chips = shares // 2
    return pl.pallas_call(
        functools.partial(hidden_kernel, groups, shares),
        out_shape=jax.ShapeDtypeStruct((slots, width), jnp.bfloat16),
        in_specs=[pl.BlockSpec(memory_space=VMEM)] * 5,
        out_specs=pl.BlockSpec(memory_space=VMEM),
        scratch_shapes=[
            VMEM((chips, tokens, width), jnp.bfloat16),
            VMEM((chips, tokens, width), jnp.bfloat16),
            VMEM((chips, tokens, width), jnp.bfloat16),
            VMEM((groups, slots, width), jnp.bfloat16),
            VMEM((groups, slots, width), jnp.bfloat16),
            VMEM((slots, 128), jnp.float32),
            VMEM((shares, slots, 128), jnp.float32),
            DMA((chips,)),
            DMA((chips,)),
            DMA((chips,)),
            DMA((chips,)),
            DMA((groups,)),
            DMA((groups,)),
            DMA((shares,)),
            DMA((shares,)),
        ],
        compiler_params=pltpu.CompilerParams(
            collective_id=1, has_side_effects=True, vmem_limit_bytes=48 * 1024 * 1024
        ),
    )(part, place, x, inv, gain)


def per_device(rollout, group_count, final_gain, head_weight, teacher_index, teacher_logprob):
    groups, shares = lax.axis_size("seq"), lax.axis_size("vocab")
    slots, features = rollout.shape
    tokens = teacher_index.shape[0]
    pack_rows = tokens // groups
    vocab_dev = head_weight.shape[1]
    own_index = lax.axis_index("seq")

    all_slots = lax.all_gather(rollout, "seq", axis=0, tiled=True)

    first_column = lax.axis_index(("seq", "vocab")) * vocab_dev
    teacher_prob = jnp.exp(teacher_logprob)
    teacher_mass = jnp.sum(teacher_prob, axis=1)
    teacher_dense = teacher_table(teacher_index - first_column, teacher_prob, vocab_dev)

    group_ids = jnp.arange(groups, dtype=jnp.int32)
    offsets = jnp.sum(jnp.where(group_ids[None, :] < group_ids[:, None], group_count[None, :], 0), axis=1)
    slot_pad = -(-slots // 8) * 8
    row_ids = jnp.arange(slot_pad, dtype=jnp.int32)
    rank = offsets[:, None] + row_ids[None, :]
    is_live = row_ids[None, :] < group_count[:, None]
    target = jnp.where(is_live, rank % groups * pack_rows + rank // groups, -1)
    token_ids = jnp.arange(tokens, dtype=jnp.int32)
    place = (target[:, :, None] == token_ids[None, None, :]).astype(jnp.bfloat16)
    gather = (target[:, :slots].reshape(1, -1) == token_ids[:, None]).astype(jnp.bfloat16)

    packed = jnp.dot(gather, all_slots, preferred_element_type=jnp.float32)
    inv_rms = lax.rsqrt(jnp.mean(packed * packed, axis=1, keepdims=True) + norm_eps)
    all_rows = (packed * inv_rms * final_gain).astype(jnp.bfloat16)
    logits = jnp.dot(all_rows, head_weight, preferred_element_type=jnp.float32)
    target_part = jnp.sum(teacher_dense * logits, axis=1)
    local_peak = jnp.max(logits, axis=1)
    local_total = jnp.sum(jnp.exp(logits - local_peak[:, None]), axis=1)
    stats = jnp.concatenate(
        [local_peak[None], local_total[None], target_part[None], jnp.zeros((5, tokens), jnp.float32)], axis=0
    )
    stats = exchange_stats(stats, groups, shares)
    log_total = stats[0] + jnp.log(stats[1])
    kl_all = jnp.sum(teacher_prob * teacher_logprob, axis=1) - stats[2] + teacher_mass * log_total
    kl = lax.dynamic_slice_in_dim(kl_all, own_index * pack_rows, pack_rows)
    student_part = teacher_mass[:, None] * jnp.exp(logits - log_total[:, None]) - teacher_dense
    grad_logits = (loss_scale * student_part).astype(jnp.bfloat16)
    part = lax.dot_general(
        grad_logits, head_weight, (((1,), (1,)), ((), ())), preferred_element_type=jnp.float32
    ).astype(jnp.bfloat16)

    share = features // shares
    feature_start = lax.axis_index("vocab") * share
    own = jnp.pad(rollout, ((0, slot_pad - slots), (0, 0)))
    own_values = own.astype(jnp.float32)
    own_inv = lax.rsqrt(jnp.mean(own_values * own_values, axis=1, keepdims=True) + norm_eps)
    own_x = lax.dynamic_slice_in_dim(own, feature_start, share, 1)
    own_gain = lax.dynamic_slice_in_dim(final_gain, feature_start, share, 0)[None, :]
    grad_rollout = reduce_hidden(part, place, own_x, own_inv, own_gain, groups, shares)[:slots]
    grad_weight = lax.dot_general(
        all_rows, grad_logits, (((0,), (0,)), ((), ())), preferred_element_type=jnp.float32
    ).astype(jnp.bfloat16)
    return (kl, grad_weight, grad_rollout)


def solution(mesh):
    placed = (P("seq", None), P(), P(), P(None, ("seq", "vocab")), P(), P())
    return jax.shard_map(
        per_device,
        mesh=mesh,
        in_specs=placed,
        out_specs=(P("seq"), P(None, ("seq", "vocab")), P("seq", "vocab")),
        check_vma=False,
    )
```

time: 384 us -> 191 us (0.50)
  waiting for transfers between devices: 121 us -> 21.4 us
  blocking collectives: 79.3 us -> 0 us
  Pallas kernels: 0 us -> 72.8 us
  other arithmetic: 83.2 us -> 15.1 us
  starting transfers between devices: 12.9 us -> 0.04 us
  local copies, waits for them, and re-layouts: 12.1 us -> 8.17 us
    reduce_scatter x1 -> x0, waiting for transfers between devices: 74.6 us -> none  [per_device(): lax.psum_scatter(lax.dot_general(grad_logits, head_weight, (((1,), (1,)),...]
    pallas_call x0 -> x3, Pallas kernels: none -> 72.8 us  [the longest x1 31.7 us: teacher_table(): pl.pallas_call(functools.partial(dense_kernel, width), grid=(tokens // 8,...]
    unnamed x4 -> x0, other arithmetic: 66.7 us -> none
    psum x1 -> x0, blocking collectives: 40.9 us -> none  [per_device(): lax.psum((local_total, target_part), ('seq', 'vocab'))]
    pmax x1 -> x0, blocking collectives: 38.4 us -> none  [per_device(): row_peak = lax.pmax(local_peak, ('seq', 'vocab'))]
    psum x1 -> x0, waiting for transfers between devices: 33.2 us -> none  [per_device(): whole_rows = lax.psum(partial_rows, 'vocab')]
    all_gather x1, waiting for transfers between devices: 0.01 us -> 20.7 us  [per_device(): all_slots = lax.all_gather(rollout, 'seq', axis=0, tiled=True)]
    all_to_all x2 -> x0, waiting for transfers between devices: 13.4 us -> none  [the longest x1 13.4 us: per_device(): lax.all_to_all(outgoing, 'seq', split_axis=1, concat_axis=1, tiled=True)]
  transfers between devices with their start and end apart: 5 -> 1, of which waited for: 3 -> 1; matrix products, arithmetic and copies ran while one was open for 24% -> 4% of each run, Pallas kernels for 0% -> 17%
where the time goes in v1:
time: 191 us; the launch traced here: 189 us
  Pallas kernels  72.8 us (38%)
  matrix products  57.4 us (30%)
  waiting for transfers between devices  21.4 us (11%)
  other arithmetic  15.1 us (8%)
  between operations  14.1 us (7%)
  local copies, waits for them, and re-layouts  8.17 us (4%)
    pallas_call x1, Pallas kernels, teacher_table(): pl.pallas_call(functools.partial(dense_kernel, width), grid=(tokens // 8,...  31.7 us
    pallas_call x1, Pallas kernels, reduce_hidden(): pl.pallas_call(functools.partial(hidden_kernel, groups, shares), out_shap...  30.1 us
    all_gather x1, waiting for transfers between devices, per_device(): all_slots = lax.all_gather(rollout, 'seq', axis=0, tiled=True)  20.7 us
    dot_general x1, matrix products, per_device(): logits = jnp.dot(all_rows, head_weight, preferred_element_type=jnp.float32)  19.9 us
    dot_general x1, matrix products, per_device(): lax.dot_general(all_rows, grad_logits, (((0,), (0,)), ((), ())), preferre...  18 us
    dot_general x1, matrix products, per_device(): lax.dot_general(grad_logits, head_weight, (((1,), (1,)), ((), ())), prefe...  16.6 us
    pallas_call x1, Pallas kernels, exchange_stats(): pl.pallas_call(functools.partial(stats_kernel, groups, shares), out_shape...  11 us
    unnamed x8, local copies, waits for them, and re-layouts  6.61 us
  transfers between devices with their start and end apart: 1, of which 1 were waited for; matrix products, arithmetic and copies ran while one was open for 4% of the time, Pallas kernels for 17%

profile of v1, /device:TPU:0, one launch (start us, length us, event | category | flops | bytes accessed | tf_op | source)
XLA Modules:
  0.0 189.0 jit_solution(3038272472985799907)
XLA Ops:
  7.2 0.0 copy-start
  7.2 0.0 all-gather.3.cloned.1.call-start
  7.2 0.7 all-gather.3.cloned.1.call-update
  7.9 0.9 copy.25
  8.8 0.8 select_reduce_fusion
  9.6 0.7 fusion.5
  10.4 0.1 eq.30
  10.4 0.9 copy.27
  11.4 1.1 multiply_reduce_fusion.2
  12.5 0.1 copy.29.inv_ref
  12.6 0.1 pad.8.clone
  12.7 0.7 dynamic_slice.11
  13.4 0.7 multiply_reduce_fusion.3
  14.1 0.6 broadcast_subtract_fusion.col_ref
  14.7 31.7 %shard_map.85 = f32[192,4752]{1,0:T(8,128)} custom-call(s32[192,64]{1,0:T(8,128)} %broadcast_subtract_fusion.col_ref, f32[192,64]{1,0:T(8,128)} %get-tuple-element.7.prob_ref), custom_call_target="tpu_custom_call" | custom-call | flops 58392576 | bytes 36495360 | tf_op jit(solution)/shard_map/pallas_call | solution.py:56
  46.4 0.0 copy-done
  46.5 0.1 fusion.place_ref
  46.6 20.7 %all-gather.3.cloned.1.call-done = bf16[8,36,4096]{2,1,0:T(8,128)(2,1)} async-done(((bf16[1,36,4096]{2,1,0:T(8,128)(2,1)}), bf16[8,36,4096]{2,1,0:T(8,128)(2,1)}) %all-gather.3.cloned.1.call-update) | async-done | bytes 2359312 | tf_op jit(solution)/shard_map/all_gather | solution.py:237
  67.3 4.1 %reshape.123 = bf16[288,4096]{1,0:T(8,128)(2,1)} reshape(bf16[8,36,4096]{2,1,0:T(8,128)(2,1)} %all-gather.3.cloned.1.call-done) | data formatting | bytes 4718592
  71.4 2.8 %multiply_reduce_fusion.1 = (f32[192]{0:T(256)S(1)}, f32[192,4096]{1,0:T(8,128)S(1)}) fusion(bf16[288,4096]{1,0:T(8,128)(2,1)} %reshape.123, s32[288]{0:T(512)S(1)} %eq.30), kind=kOutput, calls=%fused_computation.6 | convolution fusion | flops 454612800 | bytes 5506944 | tf_op jit(solution)/shard_map/dot_general | solution.py:255
  74.2 0.0 copy-done.1
  74.2 19.9 %fusion.13 = (f32[192]{0:T(256)S(1)}, f32[192,4752]{1,0:T(8,128)}) fusion(bf16[4096,4752]{0,1:T(8,128)(2,1)} %param.9, f32[192,4096]{1,0:T(8,128)S(1)} %get-tuple-element.11, f32[4096]{0:T(1024)S(1)} %copy-done.1, f32[192]{0:T(256)S(1)} %add_rsqrt_fusion), kind=kOutput, calls=%fused_computation.42 | convolution fusion | flops 7477521408 | bytes 45741568 | tf_op jit(solution)/shard_map/dot_general | solution.py:258
  94.1 4.1 %exponential_reduce_fusion = (f32[192]{0:T(256)S(1)}, f32[192]{0:T(256)S(1)}) fusion(f32[192,4752]{1,0:T(8,128)} %get-tuple-element.13, f32[192]{0:T(256)S(1)} %get-tuple-element.12, f32[192,4752]{1,0:T(8,128)} %shard_map.85), kind=kLoop, calls=%fused_computation.4 | loop fusion | flops 3649152 | bytes 7301376 | tf_op jit(solution)/shard_map/reduce_sum | solution.py:261
  98.3 0.7 maximum_maximum_fusion.in_ref
  98.9 11.0 %shard_map.86 = f32[8,192]{1,0:T(8,128)} custom-call(f32[8,192]{1,0:T(8,128)} %maximum_maximum_fusion.in_ref), custom_call_target="tpu_custom_call" | custom-call | tf_op jit(solution)/shard_map/pallas_call | solution.py:110
  110.0 0.8 fusion.12
  110.8 5.4 %multiply_convert_fusion = bf16[192,4752]{1,0:T(8,128)(2,1)} fusion(f32[192,4752]{1,0:T(8,128)} %shard_map.85, f32[192,4752]{1,0:T(8,128)} %get-tuple-element.13, f32[192]{0:T(256)S(1)} %bitcast.20, f32[192]{0:T(256)S(1)} %get-tuple-element.6), kind=kLoop, calls=%fused_computation.2 | loop fusion | flops 4561920 | bytes 9125376 | tf_op jit(solution)/shard_map/convert_element_type | solution.py:270
  116.2 18.0 %convolution_convert_fusion = bf16[4096,4752]{0,1:T(8,128)(2,1)} fusion(bf16[192,4752]{1,0:T(8,128)(2,1)} %multiply_convert_fusion, f32[192,4096]{1,0:T(8,128)S(1)} %get-tuple-element.11, f32[4096]{0:T(1024)S(1)} %copy-done.1, f32[192]{0:T(256)S(1)} %add_rsqrt_fusion), kind=kOutput, calls=%fused_computation | convolution fusion | flops 7496073216 | bytes 43916032 | tf_op jit(solution)/shard_map/dot_general | solution.py:283
  134.2 16.6 %convolution_convert_fusion.1.part_ref = bf16[192,4096]{1,0:T(8,128)(2,1)S(1)} fusion(bf16[192,4752]{1,0:T(8,128)(2,1)} %multiply_convert_fusion, bf16[4096,4752]{0,1:T(8,128)(2,1)} %param.9), kind=kOutput, calls=%fused_computation.1 | convolution fusion | flops 7475036160 | bytes 42326016 | tf_op jit(solution)/shard_map/dot_general | solution.py:271
  150.9 30.1 %shard_map.87 = bf16[40,1024]{1,0:T(8,128)(2,1)S(1)} custom-call(bf16[192,4096]{1,0:T(8,128)(2,1)S(1)} %convolution_convert_fusion.1.part_ref, bf16[8,40,192]{2,1,0:T(8,128)(2,1)S(1)} %fusion.place_ref, bf16[40,1024]{1,0:T(8,128)(2,1)S(1)} %pad_dynamic-slice_fusion.x_ref, f32[40,1]{1,0:T(8,128)S(1)} %copy.29.inv_ref, f32[1,1024]{1,0:T(1,128)S(1)} %bitcast.17), custom_call_target="tpu_custom_call" | custom-call | tf_op jit(solution)/shard_map/pallas_call | solution.py:201
  181.0 0.6 dynamic_slice.9
  181.5 0.6 copy.31
  (6 shorter events, 0.0 us)
Async XLA Ops:
  7.2 39.3 %copy-start = (bf16[36,4096]{1,0:T(8,128)(2,1)S(1)}, bf16[36,4096]{1,0:T(8,128)(2,1)}, u32[]{:S(2)}) copy-start(bf16[36,4096]{1,0:T(8,128)(2,1)} %param.6) | copy-start | bytes 884740
  7.2 60.1 %all-gather.3.cloned.1.call-start = ((), (), s32[]{:S(2)}) async-start(), calls=%async_computation | async-start | bytes 2949120 | tf_op jit(solution)/shard_map/all_gather | solution.py:237
  71.4 2.8 %copy-start.1 = (f32[4096]{0:T(1024)S(1)}, f32[4096]{0:T(1024)}, u32[]{:S(2)}) copy-start(f32[4096]{0:T(1024)} %param.8) | copy-start | bytes 49156
Sparse Core Ops, SparseCore 0:
  10.2 57.1 all-gather.2
